TPU v7x, 512 devices: a whole 4x8x8 slice. The times are simulated.
512 devices in a mesh: gx: 64 (over y_hi, z, core), gy: 8 (over x, y_lo).
Axes of the slice: x: 4, y: 8 (y_hi: 4, y_lo: 2; y = y_hi * 2 + y_lo), z: 8, core: 2. Of those that a mesh axis runs over, the one named last changes fastest.
Arguments:
- fwd_pops: bfloat16 [3, 19, 256, 64, 128], P(None, None, 'gx', 'gy'), may hold values from -4 to 4
- fwd_scale: float32 [3, 256, 64, 128], P(None, 'gx', 'gy'), may hold values from 0.01 to 0.1
- seed_adjoint: float32 [19, 256, 64, 128], P(None, 'gx', 'gy'), may hold values from -16 to 16
- turbine_map: int32 [256, 64, 128], P('gx', 'gy'), may hold values from -1 to 39, as said below
- thrust: float32 [40], replicated, may hold values from 0.4 to 0.88
Outputs:
- adjoint_out: float32 [19, 256, 64, 128], P(None, 'gx', 'gy')
- thrust_grad: float32 [40], replicated
Inputs may be any that keep to these rules, and one draw needn't show every extreme that they name: `turbine_map`: every turbine's disk is the set of cells in one streamwise plane within 4 cells (Euclidean, spanwise distance wrapping) of its centre; disks never intersect and every turbine covers cells.
All inputs are finite; a program needn't handle non-finite values.
Results may differ from a plain program's by a relative error of at most 0.0003.
Values sent between devices are 32-bit elements; how exact they have to be, the bound alone decides.
A program may use at most 64 MiB of HBM per device.

v0:
```python
import jax
import jax.numpy as jnp
from jax import lax
from jax.sharding import PartitionSpec as P

VELOCITIES = (
    (0, 0, 0),
    (1, 0, 0),
    (-1, 0, 0),
    (0, 1, 0),
    (0, -1, 0),
    (0, 0, 1),
    (0, 0, -1),
    (1, 1, 0),
    (-1, -1, 0),
    (1, -1, 0),
    (-1, 1, 0),
    (1, 0, 1),
    (-1, 0, -1),
    (1, 0, -1),
    (-1, 0, 1),
    (0, 1, 1),
    (0, -1, -1),
    (0, 1, -1),
    (0, -1, 1),
)
OPPOSITE = (0, 2, 1, 4, 3, 6, 5, 8, 7, 10, 9, 12, 11, 14, 13, 16, 15, 18, 17)
WEIGHTS = tuple([1.0 / 3.0] + [1.0 / 18.0] * 6 + [1.0 / 36.0] * 12)
MEAN_FLOW = 0.1
TAU_BASE = 0.51
SMAG_COEF = 18.0 * 1.4142135623730951 * 0.17 * 0.17
QUAD_FLOOR = 0.0001
PAIRS = ((0, 0, 1.0), (1, 1, 1.0), (2, 2, 1.0), (0, 1, 2.0), (0, 2, 2.0), (1, 2, 2.0))


def extended(block, sides, width):
    for axis, dim in sides:
        count = lax.axis_size(axis)
        forward = [(i, i + 1) for i in range(count - 1)]
        forward.append((count - 1, 0))
        backward = [(target, source) for source, target in forward]
        low = lax.ppermute(
            lax.slice_in_dim(block, block.shape[dim] - width, None, axis=dim), axis, forward
        )
        high = lax.ppermute(lax.slice_in_dim(block, 0, width, axis=dim), axis, backward)
        block = jnp.concatenate([low, block, high], axis=dim)
    return block


def base_values():
    values = []
    for member in range(19):
        along = float(VELOCITIES[member][0])
        values.append(
            WEIGHTS[member]
            * (
                1.0
                + 3.0 * MEAN_FLOW * along
                + 4.5 * MEAN_FLOW * MEAN_FLOW * along * along
                - 1.5 * MEAN_FLOW * MEAN_FLOW
            )
        )
    return values


def decode(stored, scaling):
    base = jnp.asarray(base_values(), dtype=jnp.float32)
    return base[:, None, None, None] * (1.0 + scaling[None] * stored.astype(jnp.float32))


def collide(populations, thrust_cell):
    density = populations[0]
    for member in range(1, 19):
        density = density + populations[member]
    velocity = []
    for axis_id in range(3):
        moment = jnp.zeros_like(density)
        for member in range(19):
            component = VELOCITIES[member][axis_id]
            if component != 0:
                moment = moment + float(component) * populations[member]
        velocity.append(moment / density)
    speed_sq = velocity[0] * velocity[0] + velocity[1] * velocity[1] + velocity[2] * velocity[2]
    nonequil = []
    for member in range(19):
        proj = (
            float(VELOCITIES[member][0]) * velocity[0]
            + float(VELOCITIES[member][1]) * velocity[1]
            + float(VELOCITIES[member][2]) * velocity[2]
        )
        equilib = (
            WEIGHTS[member] * density * (1.0 + 3.0 * proj + 4.5 * proj * proj - 1.5 * speed_sq)
        )
        nonequil.append(populations[member] - equilib)
    stress_sum = jnp.zeros_like(density)
    for first, second, factor in PAIRS:
        stress = jnp.zeros_like(density)
        for member in range(19):
            product = VELOCITIES[member][first] * VELOCITIES[member][second]
            if product != 0:
                stress = stress + float(product) * nonequil[member]
        stress_sum = stress_sum + factor * stress * stress
    magnitude = jnp.sqrt(stress_sum + QUAD_FLOOR)
    relaxation = 0.5 * (TAU_BASE + jnp.sqrt(TAU_BASE * TAU_BASE + SMAG_COEF * magnitude / density))
    thrust_force = -0.5 * thrust_cell * velocity[0] * jnp.abs(velocity[0])
    result = []
    for member in range(19):
        result.append(
            populations[member]
            - nonequil[member] / relaxation
            + 3.0 * WEIGHTS[member] * float(VELOCITIES[member][0]) * thrust_force
        )
    return jnp.stack(result)


def local_thrust(values):
    return 4.0 * values / jnp.square(1.0 + jnp.sqrt(1.0 - values))


def finish_vertical(shifted, adjoint):
    result = []
    for member in range(19):
        vertical = VELOCITIES[member][2]
        mirror = adjoint[OPPOSITE[member]]
        if vertical == 1:
            result.append(jnp.concatenate([shifted[member][..., 1:], mirror[..., -1:]], axis=-1))
        elif vertical == -1:
            result.append(jnp.concatenate([mirror[..., :1], shifted[member][..., :-1]], axis=-1))
        else:
            result.append(shifted[member])
    return jnp.stack(result)


def pull_whole(adjoint):
    width_x = adjoint.shape[1]
    width_y = adjoint.shape[2]
    padded = extended(adjoint, (("gx", 1), ("gy", 2)), 1)
    shifted = []
    for member in range(19):
        start_x = 1 + VELOCITIES[member][0]
        start_y = 1 + VELOCITIES[member][1]
        shifted.append(padded[member, start_x : start_x + width_x, start_y : start_y + width_y])
    return shifted


def shards(fwd_pops, fwd_scale, seed_adjoint, turbine_map, thrust):
    steps_count = fwd_pops.shape[0]
    turbines = thrust.shape[0]
    inside = turbine_map >= 0
    ids = jnp.maximum(turbine_map, 0)
    thrust_cell = jnp.where(inside, jnp.take(local_thrust(thrust), ids), 0.0)
    selector = (
        turbine_map.reshape(-1)[None, :] == jnp.arange(turbines, dtype=jnp.int32)[:, None]
    ).astype(jnp.float32)
    adjoint = seed_adjoint
    summed = jnp.zeros((turbines,), jnp.float32)
    for instant in range(steps_count - 1, -1, -1):
        shifted = pull_whole(adjoint)
        incoming = finish_vertical(shifted, adjoint)
        populations = decode(fwd_pops[instant], fwd_scale[instant])
        _, pullback = jax.vjp(collide, populations, thrust_cell)
        adjoint, cell_grad = pullback(incoming)
        partial_value = jnp.dot(selector, cell_grad.reshape(-1), precision=lax.Precision.HIGHEST)
        summed = summed + lax.psum(partial_value, ("gx", "gy"))
    _, slope = jax.vjp(local_thrust, thrust)
    thrust_grad = slope(summed)[0]
    return (adjoint, thrust_grad)


def solution(mesh):
    placed = (
        P(None, None, "gx", "gy", None),
        P(None, "gx", "gy", None),
        P(None, "gx", "gy", None),
        P("gx", "gy", None),
        P(),
    )
    return jax.shard_map(
        shards,
        mesh=mesh,
        in_specs=placed,
        out_specs=(P(None, "gx", "gy", None), P()),
        check_vma=False,
    )
```

profile of v0, /device:TPU:1, one launch (start us, length us, event | category | flops | bytes accessed | tf_op | source)
XLA Modules:
  0.0 210.3 jit_solution(3809331997882569221)
XLA Ops:
  0.6 1.0 fusion.1098
  1.6 5.4 %collective-permute-start = (f32[19,1,8,128]{3,2,1,0:T(8,128)S(1)}, f32[19,1,8,128]{3,2,1,0:T(8,128)S(1)}, u32[]{:S(2)}, u32[]{:S(2)}) collective-permute-start(f32[19,1,8,128]{3,2,1,0:T(8,128)S(1)} %get-tuple-element.324), channel_id=1, source_target_pairs={{0,8},{8,16},{16,24},{24,32},{32,40},{40,48},{48,56},{56,64},{64,7... | collective-permute-start | bytes 233480 | tf_op jit(solution)/shard_map/ppermute | solution.py:42
  7.0 5.4 %collective-permute-start.1 = (f32[19,1,8,128]{3,2,1,0:T(8,128)S(1)}, f32[19,1,8,128]{3,2,1,0:T(8,128)S(1)}, u32[]{:S(2)}, u32[]{:S(2)}) collective-permute-start(f32[19,1,8,128]{3,2,1,0:T(8,128)S(1)} %get-tuple-element.325), channel_id=1, source_target_pairs={{8,0},{16,8},{24,16},{32,24},{40,32},{48,40},{56,48},{64,56},{72,6... | collective-permute-start | bytes 233480 | tf_op jit(solution)/shard_map/ppermute | solution.py:45
  12.6 0.6 copy-done.2
  13.7 0.7 copy-done.5
  15.0 24.7 %gather_fusion = f32[4096]{0:T(1024)S(1)} fusion(f32[40]{0:T(128)S(1)} %multiply_divide_fusion, s32[4096]{0:T(1024)S(1)} %bitcast_clamp_fusion), kind=kCustom, calls=%fused_computation | custom fusion | bytes 49152 | tf_op jit(solution)/shard_map/jit(_take)/gather | solution.py:151
  40.0 2.0 collective-permute-start.3
  42.0 3.3 %collective-permute-start.2 = (f32[19,6,1,128]{3,2,1,0:T(1,128)S(1)}, f32[19,6,1,128]{3,2,1,0:T(1,128)S(1)}, u32[]{:S(2)}, u32[]{:S(2)}) collective-permute-start(f32[19,6,1,128]{3,2,1,0:T(1,128)S(1)} %get-tuple-element.262), channel_id=1, source_target_pairs={{0,1},{1,2},{2,3},{3,4},{4,5},{5,6},{6,7},{7,0},{8,9},{9,10},{10,1... | collective-permute-start | bytes 175112 | tf_op jit(solution)/shard_map/ppermute | solution.py:42
  45.4 3.6 %collective-permute-done.2 = f32[19,6,1,128]{3,2,1,0:T(1,128)S(1)} collective-permute-done((f32[19,6,1,128]{3,2,1,0:T(1,128)S(1)}, f32[19,6,1,128]{3,2,1,0:T(1,128)S(1)}, u32[]{:S(2)}, u32[]{:S(2)}) %collective-permute-start.2) | collective-permute-done | bytes 58400 | tf_op jit(solution)/shard_map/ppermute | solution.py:42
  51.5 0.6 copy-done.4
  52.3 5.2 %collective-permute-start.4 = (f32[19,1,8,128]{3,2,1,0:T(8,128)S(1)}, f32[19,1,8,128]{3,2,1,0:T(8,128)S(1)}, u32[]{:S(2)}, u32[]{:S(2)}) collective-permute-start(f32[19,1,8,128]{3,2,1,0:T(8,128)S(1)} %get-tuple-element.309), channel_id=1, source_target_pairs={{0,8},{8,16},{16,24},{24,32},{32,40},{40,48},{48,56},{56,64},{64,7... | collective-permute-start | bytes 233480 | tf_op jit(solution)/shard_map/ppermute | solution.py:42
  57.6 9.4 %collective-permute-start.5 = (f32[19,1,8,128]{3,2,1,0:T(8,128)S(1)}, f32[19,1,8,128]{3,2,1,0:T(8,128)S(1)}, u32[]{:S(2)}, u32[]{:S(2)}) collective-permute-start(f32[19,1,8,128]{3,2,1,0:T(8,128)S(1)} %get-tuple-element.310), channel_id=1, source_target_pairs={{8,0},{16,8},{24,16},{32,24},{40,32},{48,40},{56,48},{64,56},{72,6... | collective-permute-start | bytes 233480 | tf_op jit(solution)/shard_map/ppermute | solution.py:45
  68.1 1.9 collective-permute-start.7
  70.0 3.4 %collective-permute-start.6 = (f32[19,6,1,128]{3,2,1,0:T(1,128)S(1)}, f32[19,6,1,128]{3,2,1,0:T(1,128)S(1)}, u32[]{:S(2)}, u32[]{:S(2)}) collective-permute-start(f32[19,6,1,128]{3,2,1,0:T(1,128)S(1)} %get-tuple-element.258), channel_id=1, source_target_pairs={{0,1},{1,2},{2,3},{3,4},{4,5},{5,6},{6,7},{7,0},{8,9},{9,10},{10,1... | collective-permute-start | bytes 175112 | tf_op jit(solution)/shard_map/ppermute | solution.py:42
  73.9 3.2 %collective-permute-done.6 = f32[19,6,1,128]{3,2,1,0:T(1,128)S(1)} collective-permute-done((f32[19,6,1,128]{3,2,1,0:T(1,128)S(1)}, f32[19,6,1,128]{3,2,1,0:T(1,128)S(1)}, u32[]{:S(2)}, u32[]{:S(2)}) %collective-permute-start.6) | collective-permute-done | bytes 58400 | tf_op jit(solution)/shard_map/ppermute | solution.py:42
  78.8 0.5 fusion.682
  80.0 1.9 collective-permute-start.8
  82.0 10.1 %collective-permute-start.9 = (f32[19,1,8,128]{3,2,1,0:T(8,128)S(1)}, f32[19,1,8,128]{3,2,1,0:T(8,128)S(1)}, u32[]{:S(2)}, u32[]{:S(2)}) collective-permute-start(f32[19,1,8,128]{3,2,1,0:T(8,128)S(1)} %get-tuple-element.296), channel_id=1, source_target_pairs={{8,0},{16,8},{24,16},{32,24},{40,32},{48,40},{56,48},{64,56},{72,6... | collective-permute-start | bytes 233480 | tf_op jit(solution)/shard_map/ppermute | solution.py:45
  93.3 1.9 collective-permute-start.11
  95.2 3.4 %collective-permute-start.10 = (f32[19,6,1,128]{3,2,1,0:T(1,128)S(1)}, f32[19,6,1,128]{3,2,1,0:T(1,128)S(1)}, u32[]{:S(2)}, u32[]{:S(2)}) collective-permute-start(f32[19,6,1,128]{3,2,1,0:T(1,128)S(1)} %get-tuple-element.254), channel_id=1, source_target_pairs={{0,1},{1,2},{2,3},{3,4},{4,5},{5,6},{6,7},{7,0},{8,9},{9,10},{10,1... | collective-permute-start | bytes 175112 | tf_op jit(solution)/shard_map/ppermute | solution.py:42
  99.0 3.2 %collective-permute-done.10 = f32[19,6,1,128]{3,2,1,0:T(1,128)S(1)} collective-permute-done((f32[19,6,1,128]{3,2,1,0:T(1,128)S(1)}, f32[19,6,1,128]{3,2,1,0:T(1,128)S(1)}, u32[]{:S(2)}, u32[]{:S(2)}) %collective-permute-start.10) | collective-permute-done | bytes 58400 | tf_op jit(solution)/shard_map/ppermute | solution.py:42
  103.0 103.2 %psum.25 = f32[40]{0:T(128)S(1)} all-reduce(f32[40]{0:T(128)S(1)} %fusion), channel_id=1, replica_groups=mesh['gx'=64,'gy'=8] {'gx','gy'}, use_global_device_ids=true, to_apply=%region_0.1 | all-reduce | flops 40 | bytes 320 | tf_op jit(solution)/shard_map/psum | solution.py:164
  206.2 0.5 multiply_add_fusion.114
  208.9 1.4 pad_add_fusion
  (122 shorter events, 12.6 us)
Async XLA Ops:
  0.6 11.8 %copy-start = (f32[19,4,8,128]{3,2,1,0:T(8,128)S(1)}, f32[19,4,8,128]{3,2,1,0:T(8,128)}, u32[]{:S(2)}) copy-start(f32[19,4,8,128]{3,2,1,0:T(8,128)} %param.10) | copy-start | bytes 933892
  1.6 38.1 %collective-permute-start = (f32[19,1,8,128]{3,2,1,0:T(8,128)S(1)}, f32[19,1,8,128]{3,2,1,0:T(8,128)S(1)}, u32[]{:S(2)}, u32[]{:S(2)}) collective-permute-start(f32[19,1,8,128]{3,2,1,0:T(8,128)S(1)} %get-tuple-element.324), channel_id=1, source_target_pairs={{0,8},{8,16},{16,24},{24,32},{32,40},{40,48},{48,56},{56,64},{64,7... | collective-permute-start | bytes 233480 | tf_op jit(solution)/shard_map/ppermute | solution.py:42
  7.0 6.7 %copy-start.1 = (bf16[3,19,4,8,128]{4,3,2,1,0:T(8,128)(2,1)S(1)}, bf16[3,19,4,8,128]{4,3,2,1,0:T(8,128)(2,1)}, u32[]{:S(2)}) copy-start(bf16[3,19,4,8,128]{4,3,2,1,0:T(8,128)(2,1)} %param.8) | copy-start | bytes 1400836
  7.0 32.8 %collective-permute-start.1 = (f32[19,1,8,128]{3,2,1,0:T(8,128)S(1)}, f32[19,1,8,128]{3,2,1,0:T(8,128)S(1)}, u32[]{:S(2)}, u32[]{:S(2)}) collective-permute-start(f32[19,1,8,128]{3,2,1,0:T(8,128)S(1)} %get-tuple-element.325), channel_id=1, source_target_pairs={{8,0},{16,8},{24,16},{32,24},{40,32},{48,40},{56,48},{64,56},{72,6... | collective-permute-start | bytes 233480 | tf_op jit(solution)/shard_map/ppermute | solution.py:45
  12.6 0.7 copy-start.2
  12.6 0.8 copy-start.3
  13.7 0.7 copy-start.5
  14.3 0.7 copy-start.6
  40.0 5.4 %collective-permute-start.3 = (f32[19,6,1,128]{3,2,1,0:T(1,128)S(1)}, f32[19,6,1,128]{3,2,1,0:T(1,128)S(1)}, u32[]{:S(2)}, u32[]{:S(2)}) collective-permute-start(f32[19,6,1,128]{3,2,1,0:T(1,128)S(1)} %get-tuple-element.261), channel_id=1, source_target_pairs={{1,0},{2,1},{3,2},{4,3},{5,4},{6,5},{7,6},{0,7},{9,8},{10,9},{11,1... | collective-permute-start | bytes 175112 | tf_op jit(solution)/shard_map/ppermute | solution.py:45
  42.0 7.0 %collective-permute-start.2 = (f32[19,6,1,128]{3,2,1,0:T(1,128)S(1)}, f32[19,6,1,128]{3,2,1,0:T(1,128)S(1)}, u32[]{:S(2)}, u32[]{:S(2)}) collective-permute-start(f32[19,6,1,128]{3,2,1,0:T(1,128)S(1)} %get-tuple-element.262), channel_id=1, source_target_pairs={{0,1},{1,2},{2,3},{3,4},{4,5},{5,6},{6,7},{7,0},{8,9},{9,10},{10,1... | collective-permute-start | bytes 175112 | tf_op jit(solution)/shard_map/ppermute | solution.py:42
  51.5 0.7 copy-start.4
  52.3 15.0 %collective-permute-start.4 = (f32[19,1,8,128]{3,2,1,0:T(8,128)S(1)}, f32[19,1,8,128]{3,2,1,0:T(8,128)S(1)}, u32[]{:S(2)}, u32[]{:S(2)}) collective-permute-start(f32[19,1,8,128]{3,2,1,0:T(8,128)S(1)} %get-tuple-element.309), channel_id=1, source_target_pairs={{0,8},{8,16},{16,24},{24,32},{32,40},{40,48},{48,56},{56,64},{64,7... | collective-permute-start | bytes 233480 | tf_op jit(solution)/shard_map/ppermute | solution.py:42
  57.6 10.3 %collective-permute-start.5 = (f32[19,1,8,128]{3,2,1,0:T(8,128)S(1)}, f32[19,1,8,128]{3,2,1,0:T(8,128)S(1)}, u32[]{:S(2)}, u32[]{:S(2)}) collective-permute-start(f32[19,1,8,128]{3,2,1,0:T(8,128)S(1)} %get-tuple-element.310), channel_id=1, source_target_pairs={{8,0},{16,8},{24,16},{32,24},{40,32},{48,40},{56,48},{64,56},{72,6... | collective-permute-start | bytes 233480 | tf_op jit(solution)/shard_map/ppermute | solution.py:45
  68.1 5.8 %collective-permute-start.7 = (f32[19,6,1,128]{3,2,1,0:T(1,128)S(1)}, f32[19,6,1,128]{3,2,1,0:T(1,128)S(1)}, u32[]{:S(2)}, u32[]{:S(2)}) collective-permute-start(f32[19,6,1,128]{3,2,1,0:T(1,128)S(1)} %get-tuple-element.257), channel_id=1, source_target_pairs={{1,0},{2,1},{3,2},{4,3},{5,4},{6,5},{7,6},{0,7},{9,8},{10,9},{11,1... | collective-permute-start | bytes 175112 | tf_op jit(solution)/shard_map/ppermute | solution.py:45
  70.0 7.0 %collective-permute-start.6 = (f32[19,6,1,128]{3,2,1,0:T(1,128)S(1)}, f32[19,6,1,128]{3,2,1,0:T(1,128)S(1)}, u32[]{:S(2)}, u32[]{:S(2)}) collective-permute-start(f32[19,6,1,128]{3,2,1,0:T(1,128)S(1)} %get-tuple-element.258), channel_id=1, source_target_pairs={{0,1},{1,2},{2,3},{3,4},{4,5},{5,6},{6,7},{7,0},{8,9},{9,10},{10,1... | collective-permute-start | bytes 175112 | tf_op jit(solution)/shard_map/ppermute | solution.py:42
  80.0 12.5 %collective-permute-start.8 = (f32[19,1,8,128]{3,2,1,0:T(8,128)S(1)}, f32[19,1,8,128]{3,2,1,0:T(8,128)S(1)}, u32[]{:S(2)}, u32[]{:S(2)}) collective-permute-start(f32[19,1,8,128]{3,2,1,0:T(8,128)S(1)} %get-tuple-element.295), channel_id=1, source_target_pairs={{0,8},{8,16},{16,24},{24,32},{32,40},{40,48},{48,56},{56,64},{64,7... | collective-permute-start | bytes 233480 | tf_op jit(solution)/shard_map/ppermute | solution.py:42
  82.0 11.0 %collective-permute-start.9 = (f32[19,1,8,128]{3,2,1,0:T(8,128)S(1)}, f32[19,1,8,128]{3,2,1,0:T(8,128)S(1)}, u32[]{:S(2)}, u32[]{:S(2)}) collective-permute-start(f32[19,1,8,128]{3,2,1,0:T(8,128)S(1)} %get-tuple-element.296), channel_id=1, source_target_pairs={{8,0},{16,8},{24,16},{32,24},{40,32},{48,40},{56,48},{64,56},{72,6... | collective-permute-start | bytes 233480 | tf_op jit(solution)/shard_map/ppermute | solution.py:45
  93.3 5.8 %collective-permute-start.11 = (f32[19,6,1,128]{3,2,1,0:T(1,128)S(1)}, f32[19,6,1,128]{3,2,1,0:T(1,128)S(1)}, u32[]{:S(2)}, u32[]{:S(2)}) collective-permute-start(f32[19,6,1,128]{3,2,1,0:T(1,128)S(1)} %get-tuple-element.253), channel_id=1, source_target_pairs={{1,0},{2,1},{3,2},{4,3},{5,4},{6,5},{7,6},{0,7},{9,8},{10,9},{11,1... | collective-permute-start | bytes 175112 | tf_op jit(solution)/shard_map/ppermute | solution.py:45
  95.2 7.0 %collective-permute-start.10 = (f32[19,6,1,128]{3,2,1,0:T(1,128)S(1)}, f32[19,6,1,128]{3,2,1,0:T(1,128)S(1)}, u32[]{:S(2)}, u32[]{:S(2)}) collective-permute-start(f32[19,6,1,128]{3,2,1,0:T(1,128)S(1)} %get-tuple-element.254), channel_id=1, source_target_pairs={{0,1},{1,2},{2,3},{3,4},{4,5},{5,6},{6,7},{7,0},{8,9},{9,10},{10,1... | collective-permute-start | bytes 175112 | tf_op jit(solution)/shard_map/ppermute | solution.py:42
where the time goes:
time: 211 us; the launch traced here: 210 us
  blocking collectives  103 us (49%)
  starting transfers between devices  53.2 us (25%)
  local copies, waits for them, and re-layouts  30.7 us (15%)
  waiting for transfers between devices  11 us (5%)
  other arithmetic  9.76 us (5%)
    psum x1, blocking collectives, shards(): summed = summed + lax.psum(partial_value, ('gx', 'gy'))  103 us
    ppermute x6, starting transfers between devices, extended(): lax.ppermute(lax.slice_in_dim(block, 0, width, axis=dim), axis, backward)  30.8 us
    gather x1, local copies, waits for them, and re-layouts, shards(): thrust_cell = jnp.where(inside, jnp.take(local_thrust(thrust), ids), 0.0)  24.7 us
    ppermute x6, starting transfers between devices, extended(): lax.ppermute(lax.slice_in_dim(block, block.shape[dim] - width, None, axis...  22.5 us
    ppermute x6, waiting for transfers between devices, extended(): lax.ppermute(lax.slice_in_dim(block, block.shape[dim] - width, None, axis...  9.99 us
  transfers between devices with their start and end apart: 12, of which 5 were waited for; matrix products, arithmetic and copies ran while one was open for 13% of the time, Pallas kernels for 0%

commit v1 on v0

v1 whole, which is shorter than its diff:
```python
import functools

import jax
import jax.numpy as jnp
from jax import lax
from jax.experimental import pallas as pl
from jax.experimental.pallas import tpu as pltpu
from jax.sharding import PartitionSpec as P

MESH = pl.DeviceIdType.MESH
F32 = jnp.float32

VELOCITIES = (
    (0, 0, 0),
    (1, 0, 0),
    (-1, 0, 0),
    (0, 1, 0),
    (0, -1, 0),
    (0, 0, 1),
    (0, 0, -1),
    (1, 1, 0),
    (-1, -1, 0),
    (1, -1, 0),
    (-1, 1, 0),
    (1, 0, 1),
    (-1, 0, -1),
    (1, 0, -1),
    (-1, 0, 1),
    (0, 1, 1),
    (0, -1, -1),
    (0, 1, -1),
    (0, -1, 1),
)
OPPOSITE = (0, 2, 1, 4, 3, 6, 5, 8, 7, 10, 9, 12, 11, 14, 13, 16, 15, 18, 17)
WEIGHTS = tuple([1.0 / 3.0] + [1.0 / 18.0] * 6 + [1.0 / 36.0] * 12)
MEAN_FLOW = 0.1
TAU_BASE = 0.51
SMAG_COEF = 18.0 * 1.4142135623730951 * 0.17 * 0.17
QUAD_FLOOR = 0.0001

SLOTS = (9, 1, 11, 13, 7, 3, 15, 17, 10, 2, 12, 14, 8, 4, 16, 18, 9, 0, 5, 6)
SLOT = {member: SLOTS.index(member) for member in range(19)}
YP = SLOTS[4:9]
YM = SLOTS[12:17]
CORES = 2
Z_CHIPS = 8
Y_LO = 2

C_N = 0
C_Q = 19
C_G = 28
C_U = 31
C_RM, C_OMB, C_W12, C_UU, C_W8, C_KX, C_KXU, C_GK = range(34, 42)
N_COEF = 42


def base_values():
    values = []
    for member in range(19):
        along = float(VELOCITIES[member][0])
        values.append(
            WEIGHTS[member]
            * (
                1.0
                + 3.0 * MEAN_FLOW * along
                + 4.5 * MEAN_FLOW * MEAN_FLOW * along * along
                - 1.5 * MEAN_FLOW * MEAN_FLOW
            )
        )
    return values


def total(terms):
    terms = list(terms)
    while len(terms) > 1:
        terms = [
            terms[i] + terms[i + 1] if i + 1 < len(terms) else terms[i]
            for i in range(0, len(terms), 2)
        ]
    return terms[0]


def second_moments(pair):
    sx, sy, sz, a, b, c, d, e, f = pair
    txy, txz, tyz = a + b, c + d, e + f
    return sx, sy, sz, txy, txz, tyz, a - b, c - d, e - f


def coefficients(pops, scale, k):
    base = base_values()
    f = [base[i] + (base[i] * scale) * pops[i] for i in range(19)]
    rho = total(f)
    sums = [f[2 * p + 1] + f[2 * p + 2] for p in range(9)]
    difs = [f[2 * p + 1] - f[2 * p + 2] for p in range(9)]
    jx = (difs[0] + difs[3] + difs[4]) + (difs[5] + difs[6])
    jy = (difs[1] + difs[3] - difs[4]) + (difs[7] + difs[8])
    jz = (difs[2] + difs[5] - difs[6]) + (difs[7] - difs[8])
    inv = 1.0 / rho
    u = (jx * inv, jy * inv, jz * inv)
    u2 = u[0] * u[0] + u[1] * u[1] + u[2] * u[2]
    rest = 1.0 - 1.5 * u2
    n = [None] * 19
    third = rho * (1.0 / 3.0)
    n[0] = f[0] - third * rest
    r18 = rho * (1.0 / 18.0)
    r36 = rho * (1.0 / 36.0)
    proj = (
        u[0],
        u[1],
        u[2],
        u[0] + u[1],
        u[0] - u[1],
        u[0] + u[2],
        u[0] - u[2],
        u[1] + u[2],
        u[1] - u[2],
    )
    for p in range(9):
        even = rest + 4.5 * (proj[p] * proj[p])
        odd = 3.0 * proj[p]
        weight = r18 if p < 3 else r36
        n[2 * p + 1] = f[2 * p + 1] - weight * (even + odd)
        n[2 * p + 2] = f[2 * p + 2] - weight * (even - odd)
    pair = [n[2 * p + 1] + n[2 * p + 2] for p in range(9)]
    sx, sy, sz, txy, txz, tyz, pxy, pxz, pyz = second_moments(pair)
    pxx = sx + txy + txz
    pyy = sy + txy + tyz
    pzz = sz + txz + tyz
    square = (pxx * pxx + pyy * pyy + pzz * pzz) + 2.0 * (
        pxy * pxy + pxz * pxz + pyz * pyz
    )
    q = jnp.sqrt(square + QUAD_FLOOR)
    s = jnp.sqrt(TAU_BASE * TAU_BASE + SMAG_COEF * (q * inv))
    om = 2.0 / (TAU_BASE + s)
    a1 = (om * om) * (0.25 * SMAG_COEF) * inv / (s * q)
    a2 = a1 * (q * q) * inv
    pu = (
        pxx * u[0] + pxy * u[1] + pxz * u[2],
        pxy * u[0] + pyy * u[1] + pyz * u[2],
        pxz * u[0] + pyz * u[1] + pzz * u[2],
    )
    upu = u[0] * pu[0] + u[1] * pu[1] + u[2] * pu[2]
    trace = pxx + pyy + pzz
    quads = (
        pxx,
        pyy,
        pzz,
        pxx + pyy + 2.0 * pxy,
        pxx + pyy - 2.0 * pxy,
        pxx + pzz + 2.0 * pxz,
        pxx + pzz - 2.0 * pxz,
        pyy + pzz + 2.0 * pyz,
        pyy + pzz - 2.0 * pyz,
    )
    absu = jnp.abs(u[0])
    kx = k * absu * inv * (1.0 / 12.0)
    out = list(n)
    out += [a1 * value for value in quads]
    out += [(2.0 * a1) * value for value in pu]
    out += list(u)
    out += [
        a2 + a1 * (trace * (1.0 / 3.0) - upu),
        1.0 - om,
        om * (1.0 / 12.0),
        om * (1.0 / 36.0) * (1.0 + 1.5 * u2),
        om * 0.125,
        kx,
        kx * u[0],
        (-1.5 / 36.0) * (u[0] * absu),
    ]
    return out


def transposed(mu, co):
    sums = [mu[2 * p + 1] + mu[2 * p + 2] for p in range(9)]
    difs = [mu[2 * p + 1] - mu[2 * p + 2] for p in range(9)]
    sx, sy, sz, txy, txz, tyz, mxy, mxz, myz = second_moments(sums)
    sx, sy, sz = sx + sx, sy + sy, sz + sz
    mxx = sx + txy + txz
    myy = sy + txy + tyz
    mzz = sz + txz + tyz
    m0 = 12.0 * mu[0] + ((sx + sy + sz) + (txy + txz + tyz))
    m1x = (difs[0] + difs[0]) + (difs[3] + difs[4]) + (difs[5] + difs[6])
    m1y = (difs[1] + difs[1]) + (difs[3] - difs[4]) + (difs[7] + difs[8])
    m1z = (difs[2] + difs[2]) + (difs[5] - difs[6]) + (difs[7] - difs[8])
    big = total(mu[i] * co(C_N + i) for i in range(19))
    ux, uy, uz = co(C_U), co(C_U + 1), co(C_U + 2)
    vx = mxx * ux + mxy * uy + mxz * uz
    vy = mxy * ux + myy * uy + myz * uz
    vz = mxz * ux + myz * uy + mzz * uz
    uv = ux * vx + uy * vy + uz * vz
    w12 = co(C_W12)
    jx = w12 * (m1x + 3.0 * vx - ux * m0) - big * co(C_G) - co(C_KX) * m1x
    jy = w12 * (m1y + 3.0 * vy - uy * m0) - big * co(C_G + 1)
    jz = w12 * (m1z + 3.0 * vz - uz * m0) - big * co(C_G + 2)
    r = co(C_UU) * m0 - co(C_W8) * uv + co(C_KXU) * m1x - big * co(C_RM)
    omb = co(C_OMB)
    odd = (jx, jy, jz, jx + jy, jx - jy, jx + jz, jx - jz, jy + jz, jy - jz)
    lam = [omb * mu[0] + r]
    for p in range(9):
        even = r + big * co(C_Q + p)
        lam.append(omb * mu[2 * p + 1] + (even + odd[p]))
        lam.append(omb * mu[2 * p + 2] + (even - odd[p]))
    return lam, m1x


def kernel(
    dims,
    thrust_ref,
    pops_hbm,
    scale_hbm,
    seed_hbm,
    map_hbm,
    out_ref,
    grad_ref,
    pops,
    scale,
    tmap,
    lam,
    halo_y,
    coef,
    gm,
    gmy,
    acc,
    push,
    rows,
    kfield,
    red,
    in_sem,
    send_sem,
    recv_sem,
    gsend_sem,
    grecv_sem,
    rsend_sem,
    rrecv_sem,
):
    n_gx, n_gy = dims
    y_hi = n_gx // (Z_CHIPS * CORES)
    x_chips = n_gy // Y_LO
    gx = lax.axis_index("gx")
    gy = lax.axis_index("gy")
    steps = 3

    loads = [pltpu.make_async_copy(map_hbm, tmap, in_sem.at[0])]
    loads.append(pltpu.make_async_copy(scale_hbm, scale, in_sem.at[1]))
    for t in (2, 1, 0):
        loads.append(pltpu.make_async_copy(pops_hbm.at[t], pops.at[t], in_sem.at[2 + t]))
    for position, member in enumerate(SLOTS):
        loads.append(
            pltpu.make_async_copy(
                seed_hbm.at[member], lam.at[0, position, pl.ds(1, 4)], in_sem.at[5 + position]
            )
        )
    for copy in loads:
        copy.start()

    right, left = lax.rem(gx + 1, n_gx), lax.rem(gx + n_gx - 1, n_gx)
    up, down = lax.rem(gy + 1, n_gy), lax.rem(gy + n_gy - 1, n_gy)
    around = (
        (left, gy),
        (right, gy),
        (gx, down),
        (gx, up),
        (left, down),
        (right, up),
        (left, up),
        (right, down),
    )
    core = lax.rem(gx, CORES)
    z = lax.rem(gx // CORES, Z_CHIPS)
    yh = gx // (CORES * Z_CHIPS)
    yl = lax.rem(gy, Y_LO)
    xc = gy // Y_LO

    def z_peer(d):
        other = lax.rem(z + d, Z_CHIPS)
        return other, ((yh * Z_CHIPS + other) * CORES + core, gy)

    def y_peer(d):
        other = lax.rem(yh * Y_LO + yl + d, y_hi * Y_LO)
        return other, (
            ((other // Y_LO) * Z_CHIPS + z) * CORES + core,
            xc * Y_LO + lax.rem(other, Y_LO),
        )

    def x_peer(d):
        other = lax.rem(xc * CORES + core + d, x_chips * CORES)
        return other, (
            (yh * Z_CHIPS + z) * CORES + lax.rem(other, CORES),
            (other // CORES) * Y_LO + yl,
        )

    phases = (
        (z_peer, z, Z_CHIPS),
        (y_peer, yh * Y_LO + yl, y_hi * Y_LO),
        (x_peer, xc * CORES + core, x_chips * CORES),
    )

    barrier = pltpu.get_barrier_semaphore()
    count = 0
    for device in around:
        pl.semaphore_signal(barrier, inc=1, device_id=device, device_id_type=MESH)
        count += 1
    for peer, _, size in phases:
        for d in range(1, size):
            pl.semaphore_signal(barrier, inc=1, device_id=peer(d)[1], device_id_type=MESH)
            count += 1

    shape = (8, 128)
    row = lax.broadcasted_iota(jnp.int32, shape, 0)
    lane = lax.broadcasted_iota(jnp.int32, shape, 1)
    row_one = lax.broadcasted_iota(jnp.int32, (1, 128), 1)

    loads[0].wait()

    turbines = thrust_ref.shape[0]

    def fill(x, _):
        ids = tmap[x]
        value = jnp.zeros(shape, F32)
        for m in range(turbines):
            value = jnp.where(ids == m, thrust_ref[m], value)
        side = 1.0 + jnp.sqrt(1.0 - value)
        kfield[x] = 4.0 * value / (side * side)
        gm[1, x + 1] = ids.astype(F32)
        acc[x] = jnp.zeros(shape, F32)
        return 0

    lax.fori_loop(0, 4, fill, 0)
    loads[1].wait()
    for t in (2, 1, 0):
        loads[2 + (2 - t)].wait()

    def prepare(i, _):
        t = i // 4
        x = lax.rem(i, 4)
        values = coefficients(
            [pops[t, member, x].astype(F32) for member in range(19)], scale[t, x], kfield[x]
        )
        for j, value in enumerate(values):
            coef[t, x, j] = value
        return 0

    lax.fori_loop(0, 12, prepare, 0)
    for x in range(4):
        gm[0, x + 1] = coef[0, x, C_GK]
    for copy in loads[5:]:
        copy.wait()
    pl.semaphore_wait(barrier, count)

    def halo_copies(e):
        parts = (
            (lam.at[e, 0:5, 1], lam.at[e, 0:5, 5]),
            (lam.at[e, 8:13, 4], lam.at[e, 8:13, 0]),
            (lam.at[e, 4:9, 1:5, 0:1], halo_y.at[e, 0, :, 1:5]),
            (lam.at[e, 12:17, 1:5, 7:8], halo_y.at[e, 1, :, 1:5]),
            (lam.at[e, 4, 1, 0:1], halo_y.at[e, 0, 0, 5]),
            (lam.at[e, 12, 4, 7:8], halo_y.at[e, 1, 0, 0]),
            (lam.at[e, 0, 1, 7:8], halo_y.at[e, 1, 4, 5]),
            (lam.at[e, 8, 4, 0:1], halo_y.at[e, 0, 4, 0]),
        )
        return [
            pltpu.make_async_remote_copy(
                src_ref=src,
                dst_ref=dst,
                send_sem=send_sem.at[e * 8 + i],
                recv_sem=recv_sem.at[e * 8 + i],
                device_id=around[i],
                device_id_type=MESH,
            )
            for i, (src, dst) in enumerate(parts)
        ]

    def field_copies():
        parts = (
            (gm.at[:, 1], gm.at[:, 5]),
            (gm.at[:, 4], gm.at[:, 0]),
            (gm.at[:, 1:5, 0:1], gmy.at[0, :, 1:5]),
            (gm.at[:, 1:5, 7:8], gmy.at[1, :, 1:5]),
            (gm.at[:, 1, 0:1], gmy.at[0, :, 5]),
            (gm.at[:, 4, 7:8], gmy.at[1, :, 0]),
            (gm.at[:, 1, 7:8], gmy.at[1, :, 5]),
            (gm.at[:, 4, 0:1], gmy.at[0, :, 0]),
        )
        return [
            pltpu.make_async_remote_copy(
                src_ref=src,
                dst_ref=dst,
                send_sem=gsend_sem.at[i],
                recv_sem=grecv_sem.at[i],
                device_id=around[i],
                device_id_type=MESH,
            )
            for i, (src, dst) in enumerate(parts)
        ]

    far_first = (4, 5, 6, 7, 0, 1, 2, 3)
    exchanges = [halo_copies(e) for e in range(steps)]
    fields = field_copies()
    for i in far_first:
        exchanges[0][i].start()
    for i in far_first:
        fields[i].start()

    def streamed(e, x):
        mu = []
        for member in range(19):
            cx, cy, cz = VELOCITIES[member]
            value = lam[e, SLOT[member], x + cx]
            if cy != 0:
                value = pltpu.roll(value, 7 if cy == 1 else 1, 0)
                side, group = (0, YP) if cy == 1 else (1, YM)
                edge = halo_y[e, side, group.index(member), x + cx]
                value = jnp.where(row == (7 if cy == 1 else 0), jnp.broadcast_to(edge, shape), value)
            if cz != 0:
                value = pltpu.roll(value, 127 if cz == 1 else 1, 1)
                value = jnp.where(
                    lane == (127 if cz == 1 else 0), lam[e, SLOT[OPPOSITE[member]], x], value
                )
            mu.append(value)
        return mu

    def plane(e, x):
        t = 2 - e
        result, m1x = transposed(streamed(e, x), lambda j: coef[t, x - 1, j])
        if e < 2:
            for position, member in enumerate(SLOTS):
                lam[e + 1, position, x] = result[member]
            acc[x - 1] += m1x * coef[t, x - 1, C_GK]
        else:
            for member in range(19):
                out_ref[member, x - 1] = result[member]
        return result

    def push_plane(x, value):
        zero = jnp.zeros(shape, F32)
        top, bottom = lane == 127, lane == 0
        first, last = row == 0, row == 7

        def lower(v):
            return jnp.where(top, zero, pltpu.roll(v, 127, 1))

        def raise_(v):
            return jnp.where(bottom, zero, pltpu.roll(v, 1, 1))

        push[0, x] = (
            (value[1] + value[1])
            + lower(value[11])
            + raise_(value[13])
            + jnp.where(last, zero, pltpu.roll(value[7], 7, 0))
            + jnp.where(first, zero, pltpu.roll(value[9], 1, 0))
        )
        push[1, x] = -(
            (value[2] + value[2])
            + raise_(value[12])
            + lower(value[14])
            + jnp.where(first, zero, pltpu.roll(value[8], 1, 0))
            + jnp.where(last, zero, pltpu.roll(value[10], 7, 0))
        )
        push[2, x] = jnp.where(top, value[12] - value[13], zero) + jnp.where(
            bottom, value[14] - value[11], zero
        )
        rows[0, 0, pl.ds(x - 1, 1), :] = value[7][0:1]
        rows[0, 1, pl.ds(x + 1, 1), :] = value[10][0:1]
        rows[1, 0, pl.ds(x - 1, 1), :] = value[9][7:8]
        rows[1, 1, pl.ds(x + 1, 1), :] = value[8][7:8]

    rows[...] = jnp.zeros((2, 2, 8, 128), F32)

    def step(e):
        for i in (2, 3):
            exchanges[e][i].wait_recv()

        def inner(i, _):
            result = plane(e, 2 + i)
            if e == 1:
                push_plane(2 + i, result)
            return 0

        lax.fori_loop(0, 2, inner, 0)
        for i in (0, 1, 4, 5, 6, 7):
            exchanges[e][i].wait_recv()

        def outer(i, _):
            result = plane(e, 1 + 3 * i)
            if e == 1:
                push_plane(1 + 3 * i, result)
            return 0

        lax.fori_loop(0, 2, outer, 0)
        if e < 2:
            for i in far_first:
                exchanges[e + 1][i].start()

    step(0)
    step(1)

    for copy in fields:
        copy.wait_recv()
    zero = jnp.zeros(shape, F32)
    weights, ids = [], []
    for x in range(6):
        value = zero
        if x + 1 <= 4:
            value = value + push[0, x + 1]
        if x - 1 >= 1:
            value = value + push[1, x - 1]
        if 1 <= x <= 4:
            value = (value + push[2, x]) * gm[0, x] + acc[x - 1]
        else:
            value = value * gm[0, x]
        weights.append(value)
        ids.append(gm[1, x])
    for side in range(2):
        value = rows[side, 0] - rows[side, 1]
        g = jnp.concatenate([gmy[1 - side, 0, x] for x in range(6)] + [jnp.zeros((2, 128), F32)], 0)
        m = jnp.concatenate([gmy[1 - side, 1, x] for x in range(6)] + [jnp.full((2, 128), -1.0, F32)], 0)
        weights.append(value * g)
        ids.append(m)
    collected = zero
    for m in range(turbines):
        part = total(jnp.where(ids[i] == float(m), weights[i], zero) for i in range(8))
        collected = jnp.where(lane == m, jnp.sum(part, axis=1, keepdims=True), collected)
    partial = jnp.sum(collected, axis=0, keepdims=True)

    reduced = []
    copies = []
    for phase, (peer, mine, size) in enumerate(phases):
        red[phase, mine] = partial
        started = []
        for d in range(1, size):
            _, device = peer(d)
            started.append(
                pltpu.make_async_remote_copy(
                    src_ref=red.at[phase, mine],
                    dst_ref=red.at[phase, mine],
                    send_sem=rsend_sem.at[phase, d],
                    recv_sem=rrecv_sem.at[phase, d],
                    device_id=device,
                    device_id_type=MESH,
                )
            )
        for copy in started:
            copy.start()
        copies += started
        if phase == 0:
            step(2)
        for copy in started:
            copy.wait_recv()
        partial = total(red[phase, j] for j in range(size))

    thrust = jnp.zeros((1, 128), F32)
    for m in range(turbines):
        thrust = jnp.where(row_one == m, thrust_ref[m], thrust)
    side = jnp.sqrt(1.0 - thrust)
    slope = 4.0 / (side * ((1.0 + side) * (1.0 + side)))
    grad_ref[...] = (partial * slope)[0, 0:turbines]

    for group in exchanges + [fields, copies]:
        for copy in group:
            copy.wait_send()


def shards(n_gx, n_gy, fwd_pops, fwd_scale, seed_adjoint, turbine_map, thrust):
    phase_max = max(Z_CHIPS, n_gx // (Z_CHIPS * CORES) * Y_LO, n_gy // Y_LO * CORES)
    hbm = pl.BlockSpec(memory_space=pl.ANY)
    vmem = pl.BlockSpec(memory_space=pltpu.VMEM)
    return pl.pallas_call(
        functools.partial(kernel, (n_gx, n_gy)),
        out_shape=(
            jax.ShapeDtypeStruct(seed_adjoint.shape, F32),
            jax.ShapeDtypeStruct(thrust.shape, F32),
        ),
        in_specs=[pl.BlockSpec(memory_space=pltpu.SMEM), hbm, hbm, hbm, hbm],
        out_specs=(vmem, vmem),
        scratch_shapes=[
            pltpu.VMEM(fwd_pops.shape, fwd_pops.dtype),
            pltpu.VMEM(fwd_scale.shape, F32),
            pltpu.VMEM(turbine_map.shape, jnp.int32),
            pltpu.VMEM((3, 20, 6, 8, 128), F32),
            pltpu.VMEM((3, 2, 5, 6, 1, 128), F32),
            pltpu.VMEM((3, 4, N_COEF, 8, 128), F32),
            pltpu.VMEM((2, 6, 8, 128), F32),
            pltpu.VMEM((2, 2, 6, 1, 128), F32),
            pltpu.VMEM((4, 8, 128), F32),
            pltpu.VMEM((3, 5, 8, 128), F32),
            pltpu.VMEM((2, 2, 8, 128), F32),
            pltpu.VMEM((4, 8, 128), F32),
            pltpu.VMEM((3, phase_max, 1, 128), F32),
            pltpu.SemaphoreType.DMA((25,)),
            pltpu.SemaphoreType.DMA((24,)),
            pltpu.SemaphoreType.DMA((24,)),
            pltpu.SemaphoreType.DMA((8,)),
            pltpu.SemaphoreType.DMA((8,)),
            pltpu.SemaphoreType.DMA((3, phase_max)),
            pltpu.SemaphoreType.DMA((3, phase_max)),
        ],
        compiler_params=pltpu.CompilerParams(collective_id=0, has_side_effects=True),
        name="adjoint",
    )(thrust, fwd_pops, fwd_scale, seed_adjoint, turbine_map)


def solution(mesh):
    placed = (
        P(None, None, "gx", "gy", None),
        P(None, "gx", "gy", None),
        P(None, "gx", "gy", None),
        P("gx", "gy", None),
        P(),
    )
    return jax.shard_map(
        functools.partial(shards, mesh.shape["gx"], mesh.shape["gy"]),
        mesh=mesh,
        in_specs=placed,
        out_specs=(P(None, "gx", "gy", None), P()),
        check_vma=False,
    )
```

time: 211 us -> 44.8 us (0.21)
  blocking collectives: 103 us -> 0 us
  starting transfers between devices: 53.2 us -> 0 us
  Pallas kernels: 0 us -> 41.8 us
  local copies, waits for them, and re-layouts: 30.7 us -> 2.22 us
  waiting for transfers between devices: 11 us -> 0 us
  other arithmetic: 9.76 us -> 0 us
    psum x1 -> x0, blocking collectives: 103 us -> none  [shards(): summed = summed + lax.psum(partial_value, ('gx', 'gy'))]
    ppermute x12 -> x0, starting transfers between devices: 53.2 us -> none  [the longest x6 30.8 us: extended(): lax.ppermute(lax.slice_in_dim(block, 0, width, axis=dim), axis, backward)]
    pallas_call x0 -> x1, Pallas kernels: none -> 41.8 us  [shards(): pl.pallas_call(functools.partial(kernel, (n_gx, n_gy)), out_shape=(jax.Sh...]
    gather x1 -> x0, local copies, waits for them, and re-layouts: 24.7 us -> none  [shards(): thrust_cell = jnp.where(inside, jnp.take(local_thrust(thrust), ids), 0.0)]
    ppermute x12 -> x0, waiting for transfers between devices: 11 us -> none  [the longest x6 9.99 us: extended(): lax.ppermute(lax.slice_in_dim(block, block.shape[dim] - width, None, axis...]
    add_any x12 -> x0, other arithmetic: 3.88 us -> none  [the longest x3 2.05 us: collide(): density = populations[0]]
    mul x13 -> x0, other arithmetic: 3.16 us -> none  [the longest x6 1.61 us: collide(): moment = moment + float(component) * populations[member]]
    broadcast_in_dim x6 -> x0, other arithmetic: 2.45 us -> none  [the longest x3 1.59 us: collide(): density = density + populations[member]]
  transfers between devices with their start and end apart: 12 -> 0, of which waited for: 5 -> 0; matrix products, arithmetic and copies ran while one was open for 13% -> 0% of each run, Pallas kernels for 0% -> 0%
where the time goes in v1:
time: 44.8 us; the launch traced here: 44.7 us
  Pallas kernels  41.8 us (93%)
  local copies, waits for them, and re-layouts  2.22 us (5%)
  between operations  0.65 us (1%)
    pallas_call x1, Pallas kernels, shards(): pl.pallas_call(functools.partial(kernel, (n_gx, n_gy)), out_shape=(jax.Sh...  41.8 us
    unnamed x4, local copies, waits for them, and re-layouts  2.22 us

profile of v1, /device:TPU:1, one launch (start us, length us, event | category | flops | bytes accessed | tf_op | source)
XLA Modules:
  0.0 44.7 jit_solution(5325193122741088109)
XLA Ops:
  0.6 41.8 %adjoint.1 = (f32[19,4,8,128]{3,2,1,0:T(8,128)}, f32[40]{0:T(128)}) custom-call(f32[40]{0:T(128)} %thrust_ref.1, bf16[3,19,4,8,128]{4,3,2,1,0:T(8,128)(2,1)} %pops_hbm.1, f32[3,4,8,128]{3,2,1,0:T(8,128)} %scale_hbm.1, f32[19,4,8,128]{3,2,1,0:T(8,128)} %seed_hbm.1, s32[4,8,128]{2,1,0:T(8,128)} %map_hbm.1), custom_call_target="tpu_custom_call" | custom-call | tf_op jit(solution)/shard_map/adjoint/pallas_call | solution.py:568
  42.4 0.0 copy-start
  42.4 1.7 %copy.9 = f32[19,4,8,128]{3,2,1,0:T(8,128)} copy(f32[19,4,8,128]{3,2,1,0:T(8,128)} %get-tuple-element.4) | data formatting | bytes 622592
  44.1 0.0 copy-done
  44.2 0.5 %copy.10 = f32[40]{0:T(128)} copy(f32[40]{0:T(128)S(1)} %copy-done) | data formatting | bytes 320
Async XLA Ops:
  42.4 1.7 %copy-start = (f32[40]{0:T(128)S(1)}, f32[40]{0:T(128)}, u32[]{:S(2)}) copy-start(f32[40]{0:T(128)} %get-tuple-element.5) | copy-start | bytes 484

commit v2 on v1

--- a/solution.py
+++ b/solution.py
@@ -206,7 +206,7 @@
 
 def kernel(
     dims,
-    thrust_ref,
+    thrust_hbm,
     pops_hbm,
     scale_hbm,
     seed_hbm,
@@ -215,6 +215,7 @@
     grad_ref,
     pops,
     scale,
+    thrust_ref,
     tmap,
     lam,
     halo_y,
@@ -241,19 +242,6 @@
     gy = lax.axis_index("gy")
     steps = 3
 
-    loads = [pltpu.make_async_copy(map_hbm, tmap, in_sem.at[0])]
-    loads.append(pltpu.make_async_copy(scale_hbm, scale, in_sem.at[1]))
-    for t in (2, 1, 0):
-        loads.append(pltpu.make_async_copy(pops_hbm.at[t], pops.at[t], in_sem.at[2 + t]))
-    for position, member in enumerate(SLOTS):
-        loads.append(
-            pltpu.make_async_copy(
-                seed_hbm.at[member], lam.at[0, position, pl.ds(1, 4)], in_sem.at[5 + position]
-            )
-        )
-    for copy in loads:
-        copy.start()
-
     right, left = lax.rem(gx + 1, n_gx), lax.rem(gx + n_gx - 1, n_gx)
     up, down = lax.rem(gy + 1, n_gy), lax.rem(gy + n_gy - 1, n_gy)
     around = (
@@ -291,16 +279,32 @@
         )
 
     phases = (
+        (x_peer, xc * CORES + core, x_chips * CORES),
         (z_peer, z, Z_CHIPS),
         (y_peer, yh * Y_LO + yl, y_hi * Y_LO),
-        (x_peer, xc * CORES + core, x_chips * CORES),
     )
 
     barrier = pltpu.get_barrier_semaphore()
     count = 0
-    for device in around:
-        pl.semaphore_signal(barrier, inc=1, device_id=device, device_id_type=MESH)
+    far_first = (4, 5, 6, 7, 0, 1, 2, 3)
+    for i in far_first:
+        pl.semaphore_signal(barrier, inc=1, device_id=around[i], device_id_type=MESH)
         count += 1
+
+    loads = [pltpu.make_async_copy(map_hbm, tmap, in_sem.at[0])]
+    loads.append(pltpu.make_async_copy(scale_hbm, scale, in_sem.at[1]))
+    for t in (2, 1, 0):
+        loads.append(pltpu.make_async_copy(pops_hbm.at[t], pops.at[t], in_sem.at[2 + t]))
+    for position, member in enumerate(SLOTS):
+        loads.append(
+            pltpu.make_async_copy(
+                seed_hbm.at[member], lam.at[0, position, pl.ds(1, 4)], in_sem.at[5 + position]
+            )
+        )
+    loads.append(pltpu.make_async_copy(thrust_hbm, thrust_ref, in_sem.at[25]))
+    for copy in loads:
+        copy.start()
+
     for peer, _, size in phases:
         for d in range(1, size):
             pl.semaphore_signal(barrier, inc=1, device_id=peer(d)[1], device_id_type=MESH)
@@ -312,6 +316,7 @@
     row_one = lax.broadcasted_iota(jnp.int32, (1, 128), 1)
 
     loads[0].wait()
+    loads[-1].wait()
 
     turbines = thrust_ref.shape[0]
 
@@ -344,7 +349,7 @@
     lax.fori_loop(0, 12, prepare, 0)
     for x in range(4):
         gm[0, x + 1] = coef[0, x, C_GK]
-    for copy in loads[5:]:
+    for copy in loads[5:-1]:
         copy.wait()
     pl.semaphore_wait(barrier, count)
 
@@ -394,7 +399,6 @@
             for i, (src, dst) in enumerate(parts)
         ]
 
-    far_first = (4, 5, 6, 7, 0, 1, 2, 3)
     exchanges = [halo_copies(e) for e in range(steps)]
     fields = field_copies()
     for i in far_first:
@@ -543,7 +547,7 @@
         for copy in started:
             copy.start()
         copies += started
-        if phase == 0:
+        if phase == len(phases) - 1:
             step(2)
         for copy in started:
             copy.wait_recv()
@@ -561,21 +565,30 @@
             copy.wait_send()
 
 
+def write_kernel(adjoint_vmem, grad_vmem, adjoint_out, grad_out, sem):
+    copies = (
+        pltpu.make_async_copy(adjoint_vmem, adjoint_out, sem.at[0]),
+        pltpu.make_async_copy(grad_vmem, grad_out, sem.at[1]),
+    )
+    for copy in copies:
+        copy.start()
+    for copy in copies:
+        copy.wait()
+
+
 def shards(n_gx, n_gy, fwd_pops, fwd_scale, seed_adjoint, turbine_map, thrust):
     phase_max = max(Z_CHIPS, n_gx // (Z_CHIPS * CORES) * Y_LO, n_gy // Y_LO * CORES)
     hbm = pl.BlockSpec(memory_space=pl.ANY)
     vmem = pl.BlockSpec(memory_space=pltpu.VMEM)
-    return pl.pallas_call(
+    results = pl.pallas_call(
         functools.partial(kernel, (n_gx, n_gy)),
-        out_shape=(
-            jax.ShapeDtypeStruct(seed_adjoint.shape, F32),
-            jax.ShapeDtypeStruct(thrust.shape, F32),
-        ),
-        in_specs=[pl.BlockSpec(memory_space=pltpu.SMEM), hbm, hbm, hbm, hbm],
+        out_shape=(pltpu.VMEM(seed_adjoint.shape, F32), pltpu.VMEM(thrust.shape, F32)),
+        in_specs=[hbm, hbm, hbm, hbm, hbm],
         out_specs=(vmem, vmem),
         scratch_shapes=[
             pltpu.VMEM(fwd_pops.shape, fwd_pops.dtype),
             pltpu.VMEM(fwd_scale.shape, F32),
+            pltpu.SMEM(thrust.shape, F32),
             pltpu.VMEM(turbine_map.shape, jnp.int32),
             pltpu.VMEM((3, 20, 6, 8, 128), F32),
             pltpu.VMEM((3, 2, 5, 6, 1, 128), F32),
@@ -587,7 +600,7 @@
             pltpu.VMEM((2, 2, 8, 128), F32),
             pltpu.VMEM((4, 8, 128), F32),
             pltpu.VMEM((3, phase_max, 1, 128), F32),
-            pltpu.SemaphoreType.DMA((25,)),
+            pltpu.SemaphoreType.DMA((26,)),
             pltpu.SemaphoreType.DMA((24,)),
             pltpu.SemaphoreType.DMA((24,)),
             pltpu.SemaphoreType.DMA((8,)),
@@ -598,6 +611,17 @@
         compiler_params=pltpu.CompilerParams(collective_id=0, has_side_effects=True),
         name="adjoint",
     )(thrust, fwd_pops, fwd_scale, seed_adjoint, turbine_map)
+    return pl.pallas_call(
+        write_kernel,
+        out_shape=(
+            jax.ShapeDtypeStruct(seed_adjoint.shape, F32),
+            jax.ShapeDtypeStruct(thrust.shape, F32),
+        ),
+        in_specs=[vmem, vmem],
+        out_specs=(hbm, hbm),
+        scratch_shapes=[pltpu.SemaphoreType.DMA((2,))],
+        name="write",
+    )(*[pltpu.with_memory_space_constraint(r, pltpu.VMEM) for r in results])
 
 
 def solution(mesh):

time: 44.8 us -> 38.1 us (0.85)
  the two profiles are of different devices: /device:TPU:1 before, /device:TPU:8 now
where the time goes in v2:
time: 38.1 us; the launch traced here: 37.9 us
  Pallas kernels  37.2 us (98%)
  between operations  0.64 us (2%)
    pallas_call x1, Pallas kernels, shards(): pl.pallas_call(functools.partial(kernel, (n_gx, n_gy)), out_shape=(pltpu....  36.5 us

profile of v2, /device:TPU:8, one launch (start us, length us, event | category | flops | bytes accessed | tf_op | source)
XLA Modules:
  0.0 37.9 jit_solution(10764729967583012770)
XLA Ops:
  0.6 36.5 %adjoint.1 = (f32[19,4,8,128]{3,2,1,0:T(8,128)S(1)}, f32[40]{0:T(128)S(1)}) custom-call(f32[40]{0:T(128)} %thrust_hbm.1, bf16[3,19,4,8,128]{4,3,2,1,0:T(8,128)(2,1)} %pops_hbm.1, f32[3,4,8,128]{3,2,1,0:T(8,128)} %scale_hbm.1, f32[19,4,8,128]{3,2,1,0:T(8,128)} %seed_hbm.1, s32[4,8,128]{2,1,0:T(8,128)} %map_hbm.1), custom_call_target="tpu_custom_call" | custom-call | tf_op jit(solution)/shard_map/adjoint/pallas_call | solution.py:583
  37.1 0.7 %write.1 = (f32[19,4,8,128]{3,2,1,0:T(8,128)}, f32[40]{0:T(128)}) custom-call(f32[19,4,8,128]{3,2,1,0:T(8,128)S(1)} %get-tuple-element.4.adjoint_vmem, f32[40]{0:T(128)S(1)} %get-tuple-element.5.grad_vmem), custom_call_target="tpu_custom_call" | custom-call | tf_op jit(solution)/shard_map/write/pallas_call | solution.py:614

commit v3 on v2

--- a/solution.py
+++ b/solution.py
@@ -234,10 +234,13 @@
     grecv_sem,
     rsend_sem,
     rrecv_sem,
+    relay_x,
+    relay_c,
+    prelay_sem,
+    frelay_sem,
+    ready_sem,
 ):
     n_gx, n_gy = dims
-    y_hi = n_gx // (Z_CHIPS * CORES)
-    x_chips = n_gy // Y_LO
     gx = lax.axis_index("gx")
     gy = lax.axis_index("gy")
     steps = 3
@@ -254,42 +257,59 @@
         (left, up),
         (right, down),
     )
-    core = lax.rem(gx, CORES)
-    z = lax.rem(gx // CORES, Z_CHIPS)
-    yh = gx // (CORES * Z_CHIPS)
+    low_size = CORES * Z_CHIPS
+    low = lax.rem(gx, low_size)
+    high = gx // low_size
+    core = lax.rem(low, CORES)
+    z = low // CORES
     yl = lax.rem(gy, Y_LO)
     xc = gy // Y_LO
 
-    def z_peer(d):
-        other = lax.rem(z + d, Z_CHIPS)
-        return other, ((yh * Z_CHIPS + other) * CORES + core, gy)
-
-    def y_peer(d):
-        other = lax.rem(yh * Y_LO + yl + d, y_hi * Y_LO)
-        return other, (
-            ((other // Y_LO) * Z_CHIPS + z) * CORES + core,
-            xc * Y_LO + lax.rem(other, Y_LO),
-        )
-
-    def x_peer(d):
-        other = lax.rem(xc * CORES + core + d, x_chips * CORES)
-        return other, (
-            (yh * Z_CHIPS + z) * CORES + lax.rem(other, CORES),
-            (other // CORES) * Y_LO + yl,
-        )
+    def x_peer(j):
+        return high * low_size + z * CORES + lax.rem(j, CORES), j // CORES * Y_LO + yl
+
+    def z_peer(j):
+        return high * low_size + j * CORES + core, gy
+
+    def y_peer(j):
+        return j // Y_LO * low_size + low, xc * Y_LO + lax.rem(j, Y_LO)
 
     phases = (
-        (x_peer, xc * CORES + core, x_chips * CORES),
+        (y_peer, high * Y_LO + yl, n_gx // low_size * Y_LO),
+        (x_peer, xc * CORES + core, n_gy // Y_LO * CORES),
         (z_peer, z, Z_CHIPS),
-        (y_peer, yh * Y_LO + yl, y_hi * Y_LO),
-    )
+    )
+
+    def far(size):
+        return sorted(range(1, size), key=lambda d: abs(d - size // 2))
+
+    is_first, is_relay, is_last = low == 0, low == 1, low == low_size - 1
+    relayed = (0, 4, 6)
+    relay_from = [(lax.rem(gx + low_size - 1, n_gx), other) for other in (gy, up, down)]
+    relay_to = (gx + low_size - 2, gy)
 
     barrier = pltpu.get_barrier_semaphore()
-    count = 0
     far_first = (4, 5, 6, 7, 0, 1, 2, 3)
-    for i in far_first:
-        pl.semaphore_signal(barrier, inc=1, device_id=around[i], device_id_type=MESH)
-        count += 1
+
+    def greet(device):
+        pl.semaphore_signal(barrier, inc=1, device_id=device, device_id_type=MESH)
+
+    @pl.when(is_relay)
+    def _():
+        for device in relay_from:
+            greet(device)
+
+    @pl.when(is_last)
+    def _():
+        greet((gx - (low_size - 2), gy))
+
+    @pl.when(jnp.logical_not(is_last))
+    def _():
+        for i in (5, 7, 1):
+            greet(around[i])
+
+    for i in (4, 6, 0, 2, 3):
+        greet(around[i])
 
     loads = [pltpu.make_async_copy(map_hbm, tmap, in_sem.at[0])]
     loads.append(pltpu.make_async_copy(scale_hbm, scale, in_sem.at[1]))
@@ -305,50 +325,16 @@
     for copy in loads:
         copy.start()
 
-    for peer, _, size in phases:
-        for d in range(1, size):
-            pl.semaphore_signal(barrier, inc=1, device_id=peer(d)[1], device_id_type=MESH)
-            count += 1
+    count = 8 + jnp.where(is_relay, 1, 0)
+    for peer, mine, size in phases:
+        lax.fori_loop(mine + 1, size, lambda j, _, peer=peer: (greet(peer(j)), 0)[1], 0)
+        count = count + mine
 
     shape = (8, 128)
     row = lax.broadcasted_iota(jnp.int32, shape, 0)
     lane = lax.broadcasted_iota(jnp.int32, shape, 1)
     row_one = lax.broadcasted_iota(jnp.int32, (1, 128), 1)
 
-    loads[0].wait()
-    loads[-1].wait()
-
-    turbines = thrust_ref.shape[0]
-
-    def fill(x, _):
-        ids = tmap[x]
-        value = jnp.zeros(shape, F32)
-        for m in range(turbines):
-            value = jnp.where(ids == m, thrust_ref[m], value)
-        side = 1.0 + jnp.sqrt(1.0 - value)
-        kfield[x] = 4.0 * value / (side * side)
-        gm[1, x + 1] = ids.astype(F32)
-        acc[x] = jnp.zeros(shape, F32)
-        return 0
-
-    lax.fori_loop(0, 4, fill, 0)
-    loads[1].wait()
-    for t in (2, 1, 0):
-        loads[2 + (2 - t)].wait()
-
-    def prepare(i, _):
-        t = i // 4
-        x = lax.rem(i, 4)
-        values = coefficients(
-            [pops[t, member, x].astype(F32) for member in range(19)], scale[t, x], kfield[x]
-        )
-        for j, value in enumerate(values):
-            coef[t, x, j] = value
-        return 0
-
-    lax.fori_loop(0, 12, prepare, 0)
-    for x in range(4):
-        gm[0, x + 1] = coef[0, x, C_GK]
     for copy in loads[5:-1]:
         copy.wait()
     pl.semaphore_wait(barrier, count)
@@ -401,10 +387,99 @@
 
     exchanges = [halo_copies(e) for e in range(steps)]
     fields = field_copies()
-    for i in far_first:
+    parked = (relay_x, relay_c.at[0], relay_c.at[1])
+
+    def relay_copy(k, src, device):
+        return pltpu.make_async_remote_copy(
+            src_ref=src,
+            dst_ref=parked[k],
+            send_sem=send_sem.at[relayed[k]],
+            recv_sem=prelay_sem.at[k],
+            device_id=device,
+            device_id_type=MESH,
+        )
+
+    sources = (lam.at[0, 0:5, 1], lam.at[0, 4, 1, 0:1], lam.at[0, 0, 1, 7:8])
+    landings = (lam.at[0, 0:5, 5], halo_y.at[0, 0, 0, 5], halo_y.at[0, 1, 4, 5])
+    inbound = []
+    forwards = []
+    for k, i in enumerate(relayed):
+        device = around[i]
+        inbound.append(relay_copy(k, sources[k], (device[0] - (low_size - 2), device[1])))
+        forwards.append(
+            pltpu.make_async_remote_copy(
+                src_ref=parked[k],
+                dst_ref=landings[k],
+                send_sem=frelay_sem.at[k],
+                recv_sem=recv_sem.at[i],
+                device_id=relay_to,
+                device_id_type=MESH,
+            )
+        )
+
+    @pl.when(is_first)
+    def _():
+        for k in (1, 2, 0):
+            inbound[k].start()
+
+    @pl.when(jnp.logical_not(is_first))
+    def _():
+        for i in (4, 6, 0):
+            exchanges[0][i].start()
+
+    for i in (5, 7, 1, 2, 3):
         exchanges[0][i].start()
-    for i in far_first:
-        fields[i].start()
+    for phase, (peer, mine, _) in enumerate(phases):
+
+        def answer(j, _, phase=phase, peer=peer):
+            pl.semaphore_signal(
+                ready_sem.at[phase], inc=1, device_id=peer(j), device_id_type=MESH
+            )
+            return 0
+
+        lax.fori_loop(0, mine, answer, 0)
+
+    @pl.when(is_relay)
+    def _():
+        for k in (1, 2, 0):
+            inbound[k].wait_recv()
+        for k in (1, 2, 0):
+            forwards[k].start()
+
+    loads[0].wait()
+    loads[-1].wait()
+
+    turbines = thrust_ref.shape[0]
+
+    def fill(x, _):
+        ids = tmap[x]
+        value = jnp.zeros(shape, F32)
+        for m in range(turbines):
+            value = jnp.where(ids == m, thrust_ref[m], value)
+        side = 1.0 + jnp.sqrt(1.0 - value)
+        kfield[x] = 4.0 * value / (side * side)
+        gm[1, x + 1] = ids.astype(F32)
+        acc[x] = jnp.zeros(shape, F32)
+        return 0
+
+    lax.fori_loop(0, 4, fill, 0)
+    loads[1].wait()
+    for t in (2, 1, 0):
+        loads[2 + (2 - t)].wait()
+
+    def prepare(i, _):
+        t = i // 4
+        x = lax.rem(i, 4)
+        values = coefficients(
+            [pops[t, member, x].astype(F32) for member in range(19)], scale[t, x], kfield[x]
+        )
+        for j, value in enumerate(values):
+            coef[t, x, j] = value
+        return 0
+
+    lax.fori_loop(0, 12, prepare, 0)
+    for x in range(4):
+        gm[0, x + 1] = coef[0, x, C_GK]
 
     def streamed(e, x):
         mu = []
@@ -497,6 +572,8 @@
                 exchanges[e + 1][i].start()
 
     step(0)
+    for i in far_first:
+        fields[i].start()
     step(1)
 
     for copy in fields:
@@ -532,8 +609,12 @@
     for phase, (peer, mine, size) in enumerate(phases):
         red[phase, mine] = partial
         started = []
-        for d in range(1, size):
-            _, device = peer(d)
+        @pl.when(mine < size - 1)
+        def _():
+            pl.semaphore_wait(ready_sem.at[phase], size - 1 - mine)
+
+        for d in far(size):
+            device = peer(lax.rem(mine + d, size))
             started.append(
                 pltpu.make_async_remote_copy(
                     src_ref=red.at[phase, mine],
@@ -562,6 +643,11 @@
 
     for group in exchanges + [fields, copies]:
         for copy in group:
+            copy.wait_send()
+
+    @pl.when(is_relay)
+    def _():
+        for copy in forwards:
             copy.wait_send()
 
 
@@ -607,6 +693,11 @@
             pltpu.SemaphoreType.DMA((8,)),
             pltpu.SemaphoreType.DMA((3, phase_max)),
             pltpu.SemaphoreType.DMA((3, phase_max)),
+            pltpu.VMEM((5, 8, 128), F32),
+            pltpu.VMEM((2, 1, 128), F32),
+            pltpu.SemaphoreType.DMA((3,)),
+            pltpu.SemaphoreType.DMA((3,)),
+            pltpu.SemaphoreType.REGULAR((3,)),
         ],
         compiler_params=pltpu.CompilerParams(collective_id=0, has_side_effects=True),
         name="adjoint",

time: 38.1 us -> 36.9 us (0.969)
  the two profiles are of different devices: /device:TPU:8 before, /device:TPU:1 now
where the time goes in v3:
time: 36.9 us; the launch traced here: 36.6 us
  Pallas kernels  35.9 us (97%)
  between operations  0.64 us (2%)
    pallas_call x1, Pallas kernels, shards(): pl.pallas_call(functools.partial(kernel, (n_gx, n_gy)), out_shape=(pltpu....  35.2 us
    pallas_call x1, Pallas kernels, shards(): pl.pallas_call(write_kernel, out_shape=(jax.ShapeDtypeStruct(seed_adjoint...  0.74 us

profile of v3, /device:TPU:1, one launch (start us, length us, event | category | flops | bytes accessed | tf_op | source)
XLA Modules:
  0.0 36.6 jit_solution(2805871344949523834)
XLA Ops:
  0.6 35.2 %adjoint.1 = (f32[19,4,8,128]{3,2,1,0:T(8,128)S(1)}, f32[40]{0:T(128)S(1)}) custom-call(f32[40]{0:T(128)} %thrust_hbm.1, bf16[3,19,4,8,128]{4,3,2,1,0:T(8,128)(2,1)} %pops_hbm.1, f32[3,4,8,128]{3,2,1,0:T(8,128)} %scale_hbm.1, f32[19,4,8,128]{3,2,1,0:T(8,128)} %seed_hbm.1, s32[4,8,128]{2,1,0:T(8,128)} %map_hbm.1), custom_call_target="tpu_custom_call" | custom-call | tf_op jit(solution)/shard_map/adjoint/pallas_call | solution.py:669
  35.8 0.7 %write.1 = (f32[19,4,8,128]{3,2,1,0:T(8,128)}, f32[40]{0:T(128)}) custom-call(f32[19,4,8,128]{3,2,1,0:T(8,128)S(1)} %get-tuple-element.4.adjoint_vmem, f32[40]{0:T(128)S(1)} %get-tuple-element.5.grad_vmem), custom_call_target="tpu_custom_call" | custom-call | tf_op jit(solution)/shard_map/write/pallas_call | solution.py:705

commit v4 on v3

--- a/solution.py
+++ b/solution.py
@@ -544,6 +544,12 @@
         rows[1, 0, pl.ds(x - 1, 1), :] = value[9][7:8]
         rows[1, 1, pl.ds(x + 1, 1), :] = value[8][7:8]
 
+    thrust = jnp.zeros((1, 128), F32)
+    for m in range(turbines):
+        thrust = jnp.where(row_one == m, thrust_ref[m], thrust)
+    side = jnp.sqrt(1.0 - thrust)
+    slope = 4.0 / (side * ((1.0 + side) * (1.0 + side)))
+
     rows[...] = jnp.zeros((2, 2, 8, 128), F32)
 
     def step(e):
@@ -630,20 +636,14 @@
         copies += started
         if phase == len(phases) - 1:
             step(2)
+            for group in exchanges + [fields, copies]:
+                for copy in group:
+                    copy.wait_send()
         for copy in started:
             copy.wait_recv()
         partial = total(red[phase, j] for j in range(size))
 
-    thrust = jnp.zeros((1, 128), F32)
-    for m in range(turbines):
-        thrust = jnp.where(row_one == m, thrust_ref[m], thrust)
-    side = jnp.sqrt(1.0 - thrust)
-    slope = 4.0 / (side * ((1.0 + side) * (1.0 + side)))
     grad_ref[...] = (partial * slope)[0, 0:turbines]
-
-    for group in exchanges + [fields, copies]:
-        for copy in group:
-            copy.wait_send()
 
     @pl.when(is_relay)
     def _():

time: 36.9 us -> 36.8 us (level)
  no operation moved by 1% of the time
where the time goes in v4:
time: 36.8 us; the launch traced here: 36.5 us
  Pallas kernels  35.8 us (97%)
  between operations  0.64 us (2%)
    pallas_call x1, Pallas kernels, shards(): pl.pallas_call(functools.partial(kernel, (n_gx, n_gy)), out_shape=(pltpu....  35.1 us
    pallas_call x1, Pallas kernels, shards(): pl.pallas_call(write_kernel, out_shape=(jax.ShapeDtypeStruct(seed_adjoint...  0.74 us

profile of v4, /device:TPU:1, one launch (start us, length us, event | category | flops | bytes accessed | tf_op | source)
XLA Modules:
  0.0 36.5 jit_solution(5862343460869590641)
XLA Ops:
  0.6 35.1 %adjoint.1 = (f32[19,4,8,128]{3,2,1,0:T(8,128)S(1)}, f32[40]{0:T(128)S(1)}) custom-call(f32[40]{0:T(128)} %thrust_hbm.1, bf16[3,19,4,8,128]{4,3,2,1,0:T(8,128)(2,1)} %pops_hbm.1, f32[3,4,8,128]{3,2,1,0:T(8,128)} %scale_hbm.1, f32[19,4,8,128]{3,2,1,0:T(8,128)} %seed_hbm.1, s32[4,8,128]{2,1,0:T(8,128)} %map_hbm.1), custom_call_target="tpu_custom_call" | custom-call | tf_op jit(solution)/shard_map/adjoint/pallas_call | solution.py:669
  35.7 0.7 %write.1 = (f32[19,4,8,128]{3,2,1,0:T(8,128)}, f32[40]{0:T(128)}) custom-call(f32[19,4,8,128]{3,2,1,0:T(8,128)S(1)} %get-tuple-element.4.adjoint_vmem, f32[40]{0:T(128)S(1)} %get-tuple-element.5.grad_vmem), custom_call_target="tpu_custom_call" | custom-call | tf_op jit(solution)/shard_map/write/pallas_call | solution.py:705
